TPU v7x, 32 devices: a whole 2x2x4 slice. The times are simulated.
32 devices in a mesh: groups: 2 (over x), seq: 16 (over z, y, core).
Axes of the slice: x: 2, y: 2, z: 4, core: 2. Of those that a mesh axis runs over, the one named last changes fastest.
Arguments:
- queries: bfloat16 [4096, 8192], P(('groups', 'seq')), parts along dimension 0, may hold values from -4.5 to 4.5
- keyvalue: bfloat16 [4096, 2048], P(('groups', 'seq')), parts along dimension 0, may hold values from -4.5 to 4.5
- doc_ids: int32 [4096], P(('groups', 'seq')), parts along dimension 0, may hold values from 0 to 7, never falling along the last dimension, each value on 1 to 512 neighbouring positions
- owner_tiles: int32 [32, 2], P(('groups', 'seq')), parts along dimension 0, may hold values from 0 to 15, as said below
- tile_counts: int32 [32], P(('groups', 'seq')), parts along dimension 0, may hold values from 0 to 2, as said below
Outputs:
- owned: bfloat16 [8192, 8192], P(('groups', 'seq')), parts along dimension 0
There are 2 independent parts, one for each index of `groups`. A program takes and returns all parts, laid end to end along the dimension named above; each array names one. Nothing has to cross between parts.
Inputs may be any that keep to these rules, and one draw needn't show every extreme that they name: `owner_tiles`: over the slots below each owner's count, every tile 0 to 15 is listed exactly once; the other slots hold 0. Tile t is listed either by its holder, the owner o with o * 128 <= t * 128 < (o + 1) * 128, or by the holder's partner, the owner whose index differs from the holder's by half the number of owners. `tile_counts`: the counts sum to 16; each is 0, 1 or 2, some owner has 2, and an owner has 2 exactly when its partner has 0.
All inputs are finite; a program needn't handle non-finite values.
Results may differ from a plain program's by a relative error of at most 0.0034.
Values may be sent and summed in bfloat16 or wider, within the bound.
A program may use at most 64 MiB of HBM per device.

v0:
```python
import jax
import jax.numpy as jnp
from jax import lax
from jax.sharding import PartitionSpec as P

QUERY_HEADS = 64
KEY_VALUE_HEADS = 8
HEAD_WIDTH = 128
TILE = 128
DOCUMENT_LIMIT = 512


def from_behind(shard, axis, by):
    count = lax.axis_size(axis)
    pairs = [(i, i + by) for i in range(count) if 0 <= i + by < count]
    return lax.ppermute(shard, axis, pairs)


def attend(queries, keys, value_rows, allowed):
    scale = queries.shape[-1] ** (-0.5)
    scores = jnp.einsum("rhgd,khd->hgrk", queries, keys, preferred_element_type=jnp.float32) * scale
    scores = jnp.where(allowed[None, None], scores, -jnp.inf)
    row_top = jnp.max(scores, axis=3, keepdims=True)
    exponent = jnp.exp(scores - row_top)
    totals = jnp.sum(exponent, axis=3, keepdims=True)
    weights = exponent.astype(jnp.bfloat16)
    mixed_rows = jnp.einsum(
        "hgrk,khd->rhgd", weights, value_rows, preferred_element_type=jnp.float32
    )
    return (mixed_rows / jnp.transpose(totals, (2, 0, 1, 3))).astype(jnp.bfloat16)


def deliver_owners(head_rows, all_lists, owner_tiles, seq_count, width):
    slots_dev = owner_tiles.shape[1]
    slot_rows = slots_dev * TILE
    tile_rows = jnp.arange(TILE, dtype=jnp.int32)
    row_index = jnp.transpose(all_lists)[:, None, :] * TILE + tile_rows[None, :, None]
    send_rows = jnp.take(head_rows, row_index.reshape(slot_rows, seq_count), axis=0)
    received = lax.all_to_all(send_rows, "seq", split_axis=1, concat_axis=1, tiled=True)
    return received.reshape(slot_rows, width)


def local(queries, keyvalue, doc_ids, owner_tiles, tile_counts):
    seq_count = lax.axis_size("seq")
    token_per_holder = queries.shape[0]
    width = queries.shape[1]
    head_share = QUERY_HEADS // seq_count
    group_width = QUERY_HEADS // KEY_VALUE_HEADS
    head_cols = head_share * HEAD_WIDTH
    slots_dev = owner_tiles.shape[1]
    reach_devs = (DOCUMENT_LIMIT - 1) // token_per_holder + 1
    doc_marks = doc_ids + 1
    kv_parts = [keyvalue]
    mark_parts = [doc_marks]
    for shift_by in range(1, reach_devs + 1):
        far_kv, far_marks = from_behind((keyvalue, doc_marks), "seq", shift_by)
        kv_parts.insert(0, far_kv)
        mark_parts.insert(0, far_marks)
    kv_near = jnp.concatenate(kv_parts, axis=0)
    near_marks = jnp.concatenate(mark_parts, axis=0)
    near_rows = kv_near.shape[0]
    keyvalue_grouped = kv_near.reshape(near_rows, KEY_VALUE_HEADS, 2, HEAD_WIDTH)
    q_place = jnp.arange(token_per_holder, dtype=jnp.int32) + reach_devs * token_per_holder
    k_place = jnp.arange(near_rows, dtype=jnp.int32)
    allowed = (doc_marks[:, None] == near_marks[None, :]) & (k_place[None, :] <= q_place[:, None])
    local_out = attend(
        queries.reshape(token_per_holder, KEY_VALUE_HEADS, group_width, HEAD_WIDTH),
        keyvalue_grouped[:, :, 0],
        keyvalue_grouped[:, :, 1],
        allowed,
    )
    local_out = local_out.reshape(token_per_holder, width)
    all_lists = lax.all_gather(owner_tiles, "seq", axis=0, tiled=True)
    out_send = local_out.reshape(token_per_holder, seq_count, head_cols)
    head_rows = lax.all_to_all(out_send, "seq", split_axis=1, concat_axis=0, tiled=True).reshape(
        token_per_holder * seq_count, head_cols
    )
    owned = deliver_owners(head_rows, all_lists, owner_tiles, seq_count, width)
    live = jnp.repeat(jnp.arange(slots_dev, dtype=jnp.int32) < tile_counts[0], TILE)
    return jnp.where(live[:, None], owned, jnp.zeros((), jnp.bfloat16))


def solution(mesh):
    placed = (
        P(("groups", "seq"), None),
        P(("groups", "seq"), None),
        P(("groups", "seq")),
        P(("groups", "seq"), None),
        P(("groups", "seq")),
    )
    return jax.shard_map(
        local, mesh=mesh, in_specs=placed, out_specs=P(("groups", "seq"), None), check_vma=False
    )
```

profile of v0, /device:TPU:15, one launch (start us, length us, event | category | flops | bytes accessed | tf_op | source)
XLA Modules:
  0.0 285.1 jit_solution(12777522837619255446)
XLA Ops:
  0.0 0.7 broadcast_add_fusion
  0.7 3.2 %collective-permute-start.4 = (s32[128]{0:T(128)S(1)}, s32[128]{0:T(128)S(1)}, u32[]{:S(2)}, u32[]{:S(2)}) collective-permute-start(s32[128]{0:T(128)S(1)} %broadcast_add_fusion), channel_id=1, source_target_pairs={{0,4},{1,5},{2,6},{3,7},{4,8},{5,9},{6,10},{7,11},{8,12},{9,13},{1... | collective-permute-start | bytes 1544 | tf_op jit(solution)/shard_map/ppermute | solution.py:16
  3.9 4.0 %collective-permute-start.5 = (s32[128]{0:T(128)S(1)}, s32[128]{0:T(128)S(1)}, u32[]{:S(2)}, u32[]{:S(2)}) collective-permute-start(s32[128]{0:T(128)S(1)} %broadcast_add_fusion), channel_id=1, source_target_pairs={{0,3},{1,4},{2,5},{3,6},{4,7},{5,8},{6,9},{7,10},{8,11},{9,12},{10... | collective-permute-start | bytes 1544 | tf_op jit(solution)/shard_map/ppermute | solution.py:16
  8.0 1.9 collective-permute-start.6
  9.9 3.4 %collective-permute-start.7 = (s32[128]{0:T(128)S(1)}, s32[128]{0:T(128)S(1)}, u32[]{:S(2)}, u32[]{:S(2)}) collective-permute-start(s32[128]{0:T(128)S(1)} %broadcast_add_fusion), channel_id=1, source_target_pairs={{0,1},{1,2},{2,3},{3,4},{4,5},{5,6},{6,7},{7,8},{8,9},{9,10},{10,1... | collective-permute-start | bytes 1544 | tf_op jit(solution)/shard_map/ppermute | solution.py:16
  13.3 1.3 copy.52
  14.6 1.9 collective-permute-start
  16.6 2.2 copy.71
  18.8 1.9 collective-permute-start.1
  20.7 1.9 collective-permute-start.2
  22.7 2.2 collective-permute-start.3
  24.9 0.2 fusion.11
  25.1 5.3 %collective-permute-done = bf16[128,2048]{0,1:T(8,128)(2,1)S(1)} collective-permute-done((bf16[128,2048]{0,1:T(8,128)(2,1)S(1)}, bf16[128,2048]{0,1:T(8,128)(2,1)S(1)}, u32[]{:S(2)}, u32[]{:S(2)}) %collective-permute-start) | collective-permute-done | bytes 524320 | tf_op jit(solution)/shard_map/ppermute | solution.py:16
  30.5 9.0 %collective-permute-done.1 = bf16[128,2048]{0,1:T(8,128)(2,1)S(1)} collective-permute-done((bf16[128,2048]{0,1:T(8,128)(2,1)S(1)}, bf16[128,2048]{0,1:T(8,128)(2,1)S(1)}, u32[]{:S(2)}, u32[]{:S(2)}) %collective-permute-start.1) | collective-permute-done | bytes 524320 | tf_op jit(solution)/shard_map/ppermute | solution.py:16
  39.6 10.8 %collective-permute-done.2 = bf16[128,2048]{0,1:T(8,128)(2,1)S(1)} collective-permute-done((bf16[128,2048]{0,1:T(8,128)(2,1)S(1)}, bf16[128,2048]{0,1:T(8,128)(2,1)S(1)}, u32[]{:S(2)}, u32[]{:S(2)}) %collective-permute-start.2) | collective-permute-done | bytes 524320 | tf_op jit(solution)/shard_map/ppermute | solution.py:16
  50.6 5.5 %collective-permute-done.3 = bf16[128,2048]{0,1:T(8,128)(2,1)S(1)} collective-permute-done((bf16[128,2048]{0,1:T(8,128)(2,1)S(1)}, bf16[128,2048]{0,1:T(8,128)(2,1)S(1)}, u32[]{:S(2)}, u32[]{:S(2)}) %collective-permute-start.3) | collective-permute-done | bytes 524320 | tf_op jit(solution)/shard_map/ppermute | solution.py:16
  56.2 0.1 constant_dynamic-update-slice_fusion
  56.4 1.5 copy-done.1
  57.8 5.9 %fusion.2 = (f32[8,8,128]{2,1,0:T(8,128)S(1)}, f32[8,640,128,8]{2,1,3,0:T(8,128)S(1)}) fusion(pred[128,640]{0,1:T(8,128)(4,1)S(1)} %fusion.11, bf16[128,8,8,128]{3,2,1,0:T(8,128)(2,1)S(1)} %bitcast.69, bf16[640,8,2,128]{0,3,2,1:T(8,128)(2,1)} %bitcast.71), kind=kOutput, calls=%fused_computation.5 | convolution fusion | flops 1357897728 | bytes 24494080 | tf_op jit(solution)/shard_map/rhgd,khd->hgrk/dot_general | solution.py:21
  63.8 5.7 %fusion = f32[8,8,128]{2,1,0:T(8,128)} fusion(f32[8,640,128,8]{2,1,3,0:T(8,128)S(1)} %get-tuple-element.6, f32[8,8,128]{2,1,0:T(8,128)S(1)} %get-tuple-element.5, pred[128,640]{0,1:T(8,128)(4,1)S(1)} %fusion.11), kind=kLoop, calls=%fused_computation.3 | loop fusion | flops 20963328 | bytes 21118976 | tf_op jit(solution)/shard_map/reduce_sum | solution.py:25
  69.5 7.8 %fusion.6 = bf16[128,8,8,128]{0,3,2,1:T(8,128)(2,1)} fusion(f32[8,640,128,8]{2,1,3,0:T(8,128)S(1)} %get-tuple-element.6, f32[8,8,128]{2,1,0:T(8,128)S(1)} %get-tuple-element.5, pred[128,640]{0,1:T(8,128)(4,1)} %copy-done.2, f32[128,8,8]{0,2,1:T(8,128)} %bitcast.76, bf16[640,8,2,128]{0,3,2,1:T(8,128)(2,1)} %bitcast.72), kind=kOutput, calls=%fused_computation.10 | convolution fusion | flops 1365245952 | bytes 24526848 | tf_op jit(solution)/shard_map/hgrk,khd->rhgd/dot_general | solution.py:27
  77.2 6.8 %all-to-all-start = ((bf16[128,16,512]{0,2,1:T(8,128)(2,1)}), bf16[128,16,512]{0,2,1:T(8,128)(2,1)S(1)}, u32[]{:S(2)}, u32[]{:S(2)}) async-start(bf16[128,16,512]{0,2,1:T(8,128)(2,1)} %bitcast.74), calls=%async_computation | async-start | bytes 4194304 | tf_op jit(solution)/shard_map/all_to_all | solution.py:75
  84.1 56.9 %all-gather = s32[16,1,2]{2,1,0:T(1,128)S(1)} all-gather(s32[1,1,2]{2,1,0:T(1,128)S(1)} %bitcast.77), channel_id=1, replica_groups=mesh['groups'=2,'seq'=16] {'seq'}, dimensions={0}, use_global_device_ids=true | all-gather | bytes 136 | tf_op jit(solution)/shard_map/all_gather | solution.py:73
  141.4 1.3 copy-done
  142.7 2.9 %copy.61 = bf16[16,128,1,512]{3,1,0,2:T(8,128)(2,1)S(1)} copy(bf16[16,128,1,512]{1,3,0,2:T(8,128)(2,1)} %bitcast.70) | data formatting | bytes 4194304 | tf_op jit(solution)/shard_map/all_to_all | solution.py:75
  145.5 17.3 %gather_fusion = bf16[4096,512]{1,0:T(8,128)(2,1)} fusion(bf16[2048,512]{1,0:T(8,128)(2,1)S(1)} %bitcast.67, s32[4096]{0:T(1024)S(1)} %broadcast_clamp_fusion), kind=kCustom, calls=%fused_computation | custom fusion | bytes 8404992 | tf_op jit(solution)/shard_map/jit(_take)/gather | solution.py:38
  162.9 7.5 %copy_select_fusion = bf16[256,16,512]{2,0,1:T(8,128)(2,1)} fusion(bf16[256,16,512]{2,1,0:T(8,128)(2,1)} %bitcast.68, pred[256,16]{0,1:T(8,128)(4,1)S(1)} %compare_and_fusion), kind=kLoop, calls=%fused_computation.11 | loop fusion | flops 2097152 | bytes 8392704 | tf_op jit(solution)/shard_map/jit(_take)/select_n | solution.py:38
  170.4 4.9 %all-to-all-start.1 = ((bf16[256,16,512]{2,0,1:T(8,128)(2,1)}), bf16[256,16,512]{2,0,1:T(8,128)(2,1)}, u32[]{:S(2)}, u32[]{:S(2)}) async-start(bf16[256,16,512]{2,0,1:T(8,128)(2,1)} %copy_select_fusion), calls=%async_computation.1 | async-start | bytes 8388608 | tf_op jit(solution)/shard_map/all_to_all | solution.py:39
  176.0 92.0 %all-to-all-done.1 = bf16[256,16,512]{2,0,1:T(8,128)(2,1)} async-done(((bf16[256,16,512]{2,0,1:T(8,128)(2,1)}), bf16[256,16,512]{2,0,1:T(8,128)(2,1)}, u32[]{:S(2)}, u32[]{:S(2)}) %all-to-all-start.1) | async-done | bytes 4194336 | tf_op jit(solution)/shard_map/all_to_all | solution.py:39
  268.0 6.4 %copy.63 = bf16[256,16,512]{0,2,1:T(8,128)(2,1)} copy(bf16[256,16,512]{2,0,1:T(8,128)(2,1)} %all-to-all-done.1) | data formatting | bytes 8388608 | tf_op jit(solution)/shard_map/all_to_all | solution.py:39
  274.4 4.4 %bitcast_select_fusion.1 = bf16[256,8192]{0,1:T(8,128)(2,1)} fusion(bf16[256,16,512]{0,2,1:T(8,128)(2,1)} %copy.63, pred[256]{0:T(512)(128)(4,1)S(1)} %broadcast_bitcast_fusion), kind=kLoop, calls=%fused_computation.8 | loop fusion | flops 2097152 | bytes 8388864 | tf_op jit(solution)/shard_map/jit(_where)/select_n | solution.py:80
  278.8 6.3 %copy.64 = bf16[256,8192]{1,0:T(8,128)(2,1)} copy(bf16[256,8192]{0,1:T(8,128)(2,1)} %bitcast_select_fusion.1) | data formatting | bytes 8388608 | tf_op jit(solution)/shard_map/jit(_where)/select_n | solution.py:80
  (35 shorter events, 1.0 us)
Async XLA Ops:
  0.0 24.9 %copy-start.4 = (s32[128]{0:T(128)S(1)}, s32[128]{0:T(128)}, u32[]{:S(2)}) copy-start(s32[128]{0:T(128)} %param.7) | copy-start | bytes 1540
  0.7 18.0 %collective-permute-start.4 = (s32[128]{0:T(128)S(1)}, s32[128]{0:T(128)S(1)}, u32[]{:S(2)}, u32[]{:S(2)}) collective-permute-start(s32[128]{0:T(128)S(1)} %broadcast_add_fusion), channel_id=1, source_target_pairs={{0,4},{1,5},{2,6},{3,7},{4,8},{5,9},{6,10},{7,11},{8,12},{9,13},{1... | collective-permute-start | bytes 1544 | tf_op jit(solution)/shard_map/ppermute | solution.py:16
  3.9 16.8 %collective-permute-start.5 = (s32[128]{0:T(128)S(1)}, s32[128]{0:T(128)S(1)}, u32[]{:S(2)}, u32[]{:S(2)}) collective-permute-start(s32[128]{0:T(128)S(1)} %broadcast_add_fusion), channel_id=1, source_target_pairs={{0,3},{1,4},{2,5},{3,6},{4,7},{5,8},{6,9},{7,10},{8,11},{9,12},{10... | collective-permute-start | bytes 1544 | tf_op jit(solution)/shard_map/ppermute | solution.py:16
  8.0 14.7 %collective-permute-start.6 = (s32[128]{0:T(128)S(1)}, s32[128]{0:T(128)S(1)}, u32[]{:S(2)}, u32[]{:S(2)}) collective-permute-start(s32[128]{0:T(128)S(1)} %broadcast_add_fusion), channel_id=1, source_target_pairs={{0,2},{1,3},{2,4},{3,5},{4,6},{5,7},{6,8},{7,9},{8,10},{9,11},{10,... | collective-permute-start | bytes 1544 | tf_op jit(solution)/shard_map/ppermute | solution.py:16
  9.9 15.0 %collective-permute-start.7 = (s32[128]{0:T(128)S(1)}, s32[128]{0:T(128)S(1)}, u32[]{:S(2)}, u32[]{:S(2)}) collective-permute-start(s32[128]{0:T(128)S(1)} %broadcast_add_fusion), channel_id=1, source_target_pairs={{0,1},{1,2},{2,3},{3,4},{4,5},{5,6},{6,7},{7,8},{8,9},{9,10},{10,1... | collective-permute-start | bytes 1544 | tf_op jit(solution)/shard_map/ppermute | solution.py:16
  14.6 15.8 %collective-permute-start = (bf16[128,2048]{0,1:T(8,128)(2,1)S(1)}, bf16[128,2048]{0,1:T(8,128)(2,1)S(1)}, u32[]{:S(2)}, u32[]{:S(2)}) collective-permute-start(bf16[128,2048]{0,1:T(8,128)(2,1)S(1)} %copy.52), channel_id=1, source_target_pairs={{0,4},{1,5},{2,6},{3,7},{4,8},{5,9},{6,10},{7,11},{8,12},{9,13},{1... | collective-permute-start | bytes 1572872 | tf_op jit(solution)/shard_map/ppermute | solution.py:16
  18.8 20.7 %collective-permute-start.1 = (bf16[128,2048]{0,1:T(8,128)(2,1)S(1)}, bf16[128,2048]{0,1:T(8,128)(2,1)S(1)}, u32[]{:S(2)}, u32[]{:S(2)}) collective-permute-start(bf16[128,2048]{0,1:T(8,128)(2,1)S(1)} %copy.52), channel_id=1, source_target_pairs={{0,3},{1,4},{2,5},{3,6},{4,7},{5,8},{6,9},{7,10},{8,11},{9,12},{10... | collective-permute-start | bytes 1572872 | tf_op jit(solution)/shard_map/ppermute | solution.py:16
  20.7 29.8 %collective-permute-start.2 = (bf16[128,2048]{0,1:T(8,128)(2,1)S(1)}, bf16[128,2048]{0,1:T(8,128)(2,1)S(1)}, u32[]{:S(2)}, u32[]{:S(2)}) collective-permute-start(bf16[128,2048]{0,1:T(8,128)(2,1)S(1)} %copy.52), channel_id=1, source_target_pairs={{0,2},{1,3},{2,4},{3,5},{4,6},{5,7},{6,8},{7,9},{8,10},{9,11},{10,... | collective-permute-start | bytes 1572872 | tf_op jit(solution)/shard_map/ppermute | solution.py:16
  22.7 33.4 %collective-permute-start.3 = (bf16[128,2048]{0,1:T(8,128)(2,1)S(1)}, bf16[128,2048]{0,1:T(8,128)(2,1)S(1)}, u32[]{:S(2)}, u32[]{:S(2)}) collective-permute-start(bf16[128,2048]{0,1:T(8,128)(2,1)S(1)} %copy.52), channel_id=1, source_target_pairs={{0,1},{1,2},{2,3},{3,4},{4,5},{5,6},{6,7},{7,8},{8,9},{9,10},{10,1... | collective-permute-start | bytes 1572872 | tf_op jit(solution)/shard_map/ppermute | solution.py:16
  25.1 38.7 %copy-start.2 = (pred[128,640]{0,1:T(8,128)(4,1)}, pred[128,640]{0,1:T(8,128)(4,1)S(1)}, u32[]{:S(2)}) copy-start(pred[128,640]{0,1:T(8,128)(4,1)S(1)} %fusion.11) | copy-start | bytes 245764
  56.3 1.5 copy-start.1
  77.2 6.8 %copy-start.3 = (s32[1,2]{1,0:T(1,128)S(1)}, s32[1,2]{1,0:T(1,128)}, u32[]{:S(2)}) copy-start(s32[1,2]{1,0:T(1,128)} %param.8) | copy-start | bytes 28
  77.2 64.1 %all-to-all-start = ((bf16[128,16,512]{0,2,1:T(8,128)(2,1)}), bf16[128,16,512]{0,2,1:T(8,128)(2,1)S(1)}, u32[]{:S(2)}, u32[]{:S(2)}) async-start(bf16[128,16,512]{0,2,1:T(8,128)(2,1)} %bitcast.74), calls=%async_computation | async-start | bytes 4194304 | tf_op jit(solution)/shard_map/all_to_all | solution.py:75
  141.4 1.3 copy-start
  170.4 97.6 %all-to-all-start.1 = ((bf16[256,16,512]{2,0,1:T(8,128)(2,1)}), bf16[256,16,512]{2,0,1:T(8,128)(2,1)}, u32[]{:S(2)}, u32[]{:S(2)}) async-start(bf16[256,16,512]{2,0,1:T(8,128)(2,1)} %copy_select_fusion), calls=%async_computation.1 | async-start | bytes 8388608 | tf_op jit(solution)/shard_map/all_to_all | solution.py:39
where the time goes:
time: 286 us; the launch traced here: 285 us
  waiting for transfers between devices  123 us (43%)
  blocking collectives  56.9 us (20%)
  local copies, waits for them, and re-layouts  40.1 us (14%)
  starting transfers between devices  32.2 us (11%)
  other arithmetic  18.6 us (7%)
  matrix products  13.7 us (5%)
    all_to_all x1, waiting for transfers between devices, deliver_owners(): lax.all_to_all(send_rows, 'seq', split_axis=1, concat_axis=1, tiled=True)  92 us
    all_gather x1, blocking collectives, local(): all_lists = lax.all_gather(owner_tiles, 'seq', axis=0, tiled=True)  56.9 us
    ppermute x8, waiting for transfers between devices, from_behind(): return lax.ppermute(shard, axis, pairs)  30.7 us
    ppermute x8, starting transfers between devices, from_behind(): return lax.ppermute(shard, axis, pairs)  20.5 us
    gather x1, local copies, waits for them, and re-layouts, deliver_owners(): jnp.take(head_rows, row_index.reshape(slot_rows, seq_count), axis=0)  17.3 us
    dot_general x1, matrix products, attend(): jnp.einsum('hgrk,khd->rhgd', weights, value_rows, preferred_element_type=...  7.78 us
    select_n x2, other arithmetic, deliver_owners(): jnp.take(head_rows, row_index.reshape(slot_rows, seq_count), axis=0)  7.62 us
    all_to_all x1, starting transfers between devices, local(): lax.all_to_all(out_send, 'seq', split_axis=1, concat_axis=0, tiled=True)  6.8 us
  transfers between devices with their start and end apart: 10, of which 5 were waited for; matrix products, arithmetic and copies ran while one was open for 2% of the time, Pallas kernels for 0%

commit v1 on v0

--- a/solution.py
+++ b/solution.py
@@ -36,7 +36,10 @@
     tile_rows = jnp.arange(TILE, dtype=jnp.int32)
     row_index = jnp.transpose(all_lists)[:, None, :] * TILE + tile_rows[None, :, None]
     send_rows = jnp.take(head_rows, row_index.reshape(slot_rows, seq_count), axis=0)
-    received = lax.all_to_all(send_rows, "seq", split_axis=1, concat_axis=1, tiled=True)
+    received = jnp.concatenate(
+        lax.all_to_all(jnp.stack(jnp.split(send_rows, lax.axis_size("seq"), axis=1)), "seq", 0, 0),
+        axis=1,
+    )
     return received.reshape(slot_rows, width)
 
 

time: 286 us -> 296 us (1.035)
  local copies, waits for them, and re-layouts: 40.1 us -> 51.6 us
    unnamed x20 -> x35, local copies, waits for them, and re-layouts: 6.79 us -> 17.6 us
    all_to_all x1 -> x0, local copies, waits for them, and re-layouts: 6.38 us -> none  [deliver_owners(): lax.all_to_all(send_rows, 'seq', split_axis=1, concat_axis=1, tiled=True)]
    reshape x0 -> x1, local copies, waits for them, and re-layouts: none -> 6.38 us  [deliver_owners(): jnp.concatenate(lax.all_to_all(jnp.stack(jnp.split(send_rows, lax.axis_si...]
where the time goes in v1:
time: 296 us; the launch traced here: 295 us
  waiting for transfers between devices  123 us (42%)
  blocking collectives  56.9 us (19%)
  local copies, waits for them, and re-layouts  51.6 us (17%)
  starting transfers between devices  32.2 us (11%)
  other arithmetic  17.3 us (6%)
  matrix products  13.7 us (5%)
    all_to_all x1, waiting for transfers between devices, deliver_owners(): lax.all_to_all(jnp.stack(jnp.split(send_rows, lax.axis_size('seq'), axis=...  92 us
    all_gather x1, blocking collectives, local(): all_lists = lax.all_gather(owner_tiles, 'seq', axis=0, tiled=True)  56.9 us
    ppermute x8, waiting for transfers between devices, from_behind(): return lax.ppermute(shard, axis, pairs)  30.7 us
    ppermute x8, starting transfers between devices, from_behind(): return lax.ppermute(shard, axis, pairs)  20.5 us
    unnamed x35, local copies, waits for them, and re-layouts  17.6 us
    gather x1, local copies, waits for them, and re-layouts, deliver_owners(): jnp.take(head_rows, row_index.reshape(slot_rows, seq_count), axis=0)  17.3 us
    dot_general x1, matrix products, attend(): jnp.einsum('hgrk,khd->rhgd', weights, value_rows, preferred_element_type=...  7.78 us
    all_to_all x1, starting transfers between devices, local(): lax.all_to_all(out_send, 'seq', split_axis=1, concat_axis=0, tiled=True)  6.8 us
  transfers between devices with their start and end apart: 10, of which 5 were waited for; matrix products, arithmetic and copies ran while one was open for 2% of the time, Pallas kernels for 0%

profile of v1, /device:TPU:15, one launch (start us, length us, event | category | flops | bytes accessed | tf_op | source)
XLA Modules:
  0.0 295.4 jit_solution(4063693266577255053)
XLA Ops:
  0.0 0.7 broadcast_add_fusion
  0.7 3.2 %collective-permute-start.4 = (s32[128]{0:T(128)S(1)}, s32[128]{0:T(128)S(1)}, u32[]{:S(2)}, u32[]{:S(2)}) collective-permute-start(s32[128]{0:T(128)S(1)} %broadcast_add_fusion), channel_id=1, source_target_pairs={{0,4},{1,5},{2,6},{3,7},{4,8},{5,9},{6,10},{7,11},{8,12},{9,13},{1... | collective-permute-start | bytes 1544 | tf_op jit(solution)/shard_map/ppermute | solution.py:16
  3.9 4.0 %collective-permute-start.5 = (s32[128]{0:T(128)S(1)}, s32[128]{0:T(128)S(1)}, u32[]{:S(2)}, u32[]{:S(2)}) collective-permute-start(s32[128]{0:T(128)S(1)} %broadcast_add_fusion), channel_id=1, source_target_pairs={{0,3},{1,4},{2,5},{3,6},{4,7},{5,8},{6,9},{7,10},{8,11},{9,12},{10... | collective-permute-start | bytes 1544 | tf_op jit(solution)/shard_map/ppermute | solution.py:16
  8.0 1.9 collective-permute-start.6
  9.9 3.4 %collective-permute-start.7 = (s32[128]{0:T(128)S(1)}, s32[128]{0:T(128)S(1)}, u32[]{:S(2)}, u32[]{:S(2)}) collective-permute-start(s32[128]{0:T(128)S(1)} %broadcast_add_fusion), channel_id=1, source_target_pairs={{0,1},{1,2},{2,3},{3,4},{4,5},{5,6},{6,7},{7,8},{8,9},{9,10},{10,1... | collective-permute-start | bytes 1544 | tf_op jit(solution)/shard_map/ppermute | solution.py:16
  13.3 1.3 copy.72
  14.6 1.9 collective-permute-start
  16.6 2.2 copy.91
  18.8 1.9 collective-permute-start.1
  20.7 1.9 collective-permute-start.2
  22.7 2.2 collective-permute-start.3
  25.1 5.3 %collective-permute-done = bf16[128,2048]{0,1:T(8,128)(2,1)S(1)} collective-permute-done((bf16[128,2048]{0,1:T(8,128)(2,1)S(1)}, bf16[128,2048]{0,1:T(8,128)(2,1)S(1)}, u32[]{:S(2)}, u32[]{:S(2)}) %collective-permute-start) | collective-permute-done | bytes 524320 | tf_op jit(solution)/shard_map/ppermute | solution.py:16
  30.5 9.0 %collective-permute-done.1 = bf16[128,2048]{0,1:T(8,128)(2,1)S(1)} collective-permute-done((bf16[128,2048]{0,1:T(8,128)(2,1)S(1)}, bf16[128,2048]{0,1:T(8,128)(2,1)S(1)}, u32[]{:S(2)}, u32[]{:S(2)}) %collective-permute-start.1) | collective-permute-done | bytes 524320 | tf_op jit(solution)/shard_map/ppermute | solution.py:16
  39.6 10.8 %collective-permute-done.2 = bf16[128,2048]{0,1:T(8,128)(2,1)S(1)} collective-permute-done((bf16[128,2048]{0,1:T(8,128)(2,1)S(1)}, bf16[128,2048]{0,1:T(8,128)(2,1)S(1)}, u32[]{:S(2)}, u32[]{:S(2)}) %collective-permute-start.2) | collective-permute-done | bytes 524320 | tf_op jit(solution)/shard_map/ppermute | solution.py:16
  50.6 5.5 %collective-permute-done.3 = bf16[128,2048]{0,1:T(8,128)(2,1)S(1)} collective-permute-done((bf16[128,2048]{0,1:T(8,128)(2,1)S(1)}, bf16[128,2048]{0,1:T(8,128)(2,1)S(1)}, u32[]{:S(2)}, u32[]{:S(2)}) %collective-permute-start.3) | collective-permute-done | bytes 524320 | tf_op jit(solution)/shard_map/ppermute | solution.py:16
  56.4 1.5 copy-done.1
  57.8 5.9 %fusion.2 = (f32[8,8,128]{2,1,0:T(8,128)S(1)}, f32[8,640,128,8]{2,1,3,0:T(8,128)S(1)}) fusion(pred[128,640]{0,1:T(8,128)(4,1)S(1)} %fusion.11, bf16[128,8,8,128]{3,2,1,0:T(8,128)(2,1)S(1)} %bitcast.134, bf16[640,8,2,128]{0,3,2,1:T(8,128)(2,1)} %bitcast.136), kind=kOutput, calls=%fused_computation.5 | convolution fusion | flops 1357897728 | bytes 24494080 | tf_op jit(solution)/shard_map/rhgd,khd->hgrk/dot_general | solution.py:21
  63.8 5.7 %fusion = f32[8,8,128]{2,1,0:T(8,128)} fusion(f32[8,640,128,8]{2,1,3,0:T(8,128)S(1)} %get-tuple-element.6, f32[8,8,128]{2,1,0:T(8,128)S(1)} %get-tuple-element.5, pred[128,640]{0,1:T(8,128)(4,1)S(1)} %fusion.11), kind=kLoop, calls=%fused_computation.3 | loop fusion | flops 20963328 | bytes 21118976 | tf_op jit(solution)/shard_map/reduce_sum | solution.py:25
  69.5 7.8 %fusion.6 = bf16[128,8,8,128]{0,3,2,1:T(8,128)(2,1)} fusion(f32[8,640,128,8]{2,1,3,0:T(8,128)S(1)} %get-tuple-element.6, f32[8,8,128]{2,1,0:T(8,128)S(1)} %get-tuple-element.5, pred[128,640]{0,1:T(8,128)(4,1)} %copy-done.2, f32[128,8,8]{0,2,1:T(8,128)} %bitcast.141, bf16[640,8,2,128]{0,3,2,1:T(8,128)(2,1)} %bitcast.137), kind=kOutput, calls=%fused_computation.10 | convolution fusion | flops 1365245952 | bytes 24526848 | tf_op jit(solution)/shard_map/hgrk,khd->rhgd/dot_general | solution.py:27
  77.2 6.8 %all-to-all-start = ((bf16[128,16,512]{0,2,1:T(8,128)(2,1)}), bf16[128,16,512]{0,2,1:T(8,128)(2,1)S(1)}, u32[]{:S(2)}, u32[]{:S(2)}) async-start(bf16[128,16,512]{0,2,1:T(8,128)(2,1)} %bitcast.139), calls=%async_computation | async-start | bytes 4194304 | tf_op jit(solution)/shard_map/all_to_all | solution.py:78
  84.1 56.9 %all-gather = s32[16,1,2]{2,1,0:T(1,128)S(1)} all-gather(s32[1,1,2]{2,1,0:T(1,128)S(1)} %bitcast.142), channel_id=1, replica_groups=mesh['groups'=2,'seq'=16] {'seq'}, dimensions={0}, use_global_device_ids=true | all-gather | bytes 136 | tf_op jit(solution)/shard_map/all_gather | solution.py:76
  141.4 1.3 copy-done
  142.7 2.9 copy.81
  145.5 17.3 %gather_fusion = bf16[4096,512]{1,0:T(8,128)(2,1)} fusion(bf16[2048,512]{1,0:T(8,128)(2,1)S(1)} %bitcast.132, s32[4096]{0:T(1024)S(1)} %broadcast_clamp_fusion), kind=kCustom, calls=%fused_computation | custom fusion | bytes 8404992 | tf_op jit(solution)/shard_map/jit(_take)/gather | solution.py:38
  162.9 6.2 %copy_select_fusion = bf16[256,16,512]{2,0,1:T(8,128)(2,1)S(1)} fusion(bf16[256,16,512]{2,1,0:T(8,128)(2,1)} %bitcast.133, pred[256,16]{0,1:T(8,128)(4,1)S(1)} %compare_and_fusion), kind=kLoop, calls=%fused_computation.11 | loop fusion | flops 2097152 | bytes 8392704 | tf_op jit(solution)/shard_map/jit(_take)/select_n | solution.py:38
  169.1 0.7 fusion.27
  169.8 0.7 fusion.26
  180.6 4.9 %all-to-all-start.1 = ((bf16[16,256,1,512]{3,1,2,0:T(8,128)(2,1)}), bf16[16,256,1,512]{3,1,2,0:T(8,128)(2,1)}, u32[]{:S(2)}, u32[]{:S(2)}) async-start(bf16[16,256,1,512]{3,1,2,0:T(8,128)(2,1)} %fusion.12), calls=%async_computation.1 | async-start | bytes 8388608 | tf_op jit(solution)/shard_map/all_to_all | solution.py:40
  186.2 92.0 %all-to-all-done.1 = bf16[16,256,1,512]{3,1,2,0:T(8,128)(2,1)} async-done(((bf16[16,256,1,512]{3,1,2,0:T(8,128)(2,1)}), bf16[16,256,1,512]{3,1,2,0:T(8,128)(2,1)}, u32[]{:S(2)}, u32[]{:S(2)}) %all-to-all-start.1) | async-done | bytes 4194336 | tf_op jit(solution)/shard_map/all_to_all | solution.py:40
  278.2 6.4 %copy.83 = bf16[256,16,1,512]{0,3,1,2:T(8,128)(2,1)} copy(bf16[256,16,1,512]{3,0,2,1:T(8,128)(2,1)} %bitcast.41) | data formatting | bytes 8388608 | tf_op jit(solution)/shard_map/reshape | solution.py:39
  284.6 4.4 %bitcast_select_fusion.1 = bf16[256,8192]{0,1:T(8,128)(2,1)} fusion(bf16[256,16,1,512]{0,3,1,2:T(8,128)(2,1)} %copy.83, pred[256]{0:T(512)(128)(4,1)S(1)} %broadcast_bitcast_fusion), kind=kLoop, calls=%fused_computation.8 | loop fusion | flops 2097152 | bytes 8388864 | tf_op jit(solution)/shard_map/jit(_where)/select_n | solution.py:83
  289.0 6.3 %copy.84 = bf16[256,8192]{1,0:T(8,128)(2,1)} copy(bf16[256,8192]{0,1:T(8,128)(2,1)} %bitcast_select_fusion.1) | data formatting | bytes 8388608 | tf_op jit(solution)/shard_map/jit(_where)/select_n | solution.py:83
  (51 shorter events, 11.3 us)
Async XLA Ops:
  0.0 24.9 %copy-start.4 = (s32[128]{0:T(128)S(1)}, s32[128]{0:T(128)}, u32[]{:S(2)}) copy-start(s32[128]{0:T(128)} %param.7) | copy-start | bytes 1540
  0.7 18.0 %collective-permute-start.4 = (s32[128]{0:T(128)S(1)}, s32[128]{0:T(128)S(1)}, u32[]{:S(2)}, u32[]{:S(2)}) collective-permute-start(s32[128]{0:T(128)S(1)} %broadcast_add_fusion), channel_id=1, source_target_pairs={{0,4},{1,5},{2,6},{3,7},{4,8},{5,9},{6,10},{7,11},{8,12},{9,13},{1... | collective-permute-start | bytes 1544 | tf_op jit(solution)/shard_map/ppermute | solution.py:16
  3.9 16.8 %collective-permute-start.5 = (s32[128]{0:T(128)S(1)}, s32[128]{0:T(128)S(1)}, u32[]{:S(2)}, u32[]{:S(2)}) collective-permute-start(s32[128]{0:T(128)S(1)} %broadcast_add_fusion), channel_id=1, source_target_pairs={{0,3},{1,4},{2,5},{3,6},{4,7},{5,8},{6,9},{7,10},{8,11},{9,12},{10... | collective-permute-start | bytes 1544 | tf_op jit(solution)/shard_map/ppermute | solution.py:16
  8.0 14.7 %collective-permute-start.6 = (s32[128]{0:T(128)S(1)}, s32[128]{0:T(128)S(1)}, u32[]{:S(2)}, u32[]{:S(2)}) collective-permute-start(s32[128]{0:T(128)S(1)} %broadcast_add_fusion), channel_id=1, source_target_pairs={{0,2},{1,3},{2,4},{3,5},{4,6},{5,7},{6,8},{7,9},{8,10},{9,11},{10,... | collective-permute-start | bytes 1544 | tf_op jit(solution)/shard_map/ppermute | solution.py:16
  9.9 15.0 %collective-permute-start.7 = (s32[128]{0:T(128)S(1)}, s32[128]{0:T(128)S(1)}, u32[]{:S(2)}, u32[]{:S(2)}) collective-permute-start(s32[128]{0:T(128)S(1)} %broadcast_add_fusion), channel_id=1, source_target_pairs={{0,1},{1,2},{2,3},{3,4},{4,5},{5,6},{6,7},{7,8},{8,9},{9,10},{10,1... | collective-permute-start | bytes 1544 | tf_op jit(solution)/shard_map/ppermute | solution.py:16
  14.6 15.8 %collective-permute-start = (bf16[128,2048]{0,1:T(8,128)(2,1)S(1)}, bf16[128,2048]{0,1:T(8,128)(2,1)S(1)}, u32[]{:S(2)}, u32[]{:S(2)}) collective-permute-start(bf16[128,2048]{0,1:T(8,128)(2,1)S(1)} %copy.72), channel_id=1, source_target_pairs={{0,4},{1,5},{2,6},{3,7},{4,8},{5,9},{6,10},{7,11},{8,12},{9,13},{1... | collective-permute-start | bytes 1572872 | tf_op jit(solution)/shard_map/ppermute | solution.py:16
  18.8 20.7 %collective-permute-start.1 = (bf16[128,2048]{0,1:T(8,128)(2,1)S(1)}, bf16[128,2048]{0,1:T(8,128)(2,1)S(1)}, u32[]{:S(2)}, u32[]{:S(2)}) collective-permute-start(bf16[128,2048]{0,1:T(8,128)(2,1)S(1)} %copy.72), channel_id=1, source_target_pairs={{0,3},{1,4},{2,5},{3,6},{4,7},{5,8},{6,9},{7,10},{8,11},{9,12},{10... | collective-permute-start | bytes 1572872 | tf_op jit(solution)/shard_map/ppermute | solution.py:16
  20.7 29.8 %collective-permute-start.2 = (bf16[128,2048]{0,1:T(8,128)(2,1)S(1)}, bf16[128,2048]{0,1:T(8,128)(2,1)S(1)}, u32[]{:S(2)}, u32[]{:S(2)}) collective-permute-start(bf16[128,2048]{0,1:T(8,128)(2,1)S(1)} %copy.72), channel_id=1, source_target_pairs={{0,2},{1,3},{2,4},{3,5},{4,6},{5,7},{6,8},{7,9},{8,10},{9,11},{10,... | collective-permute-start | bytes 1572872 | tf_op jit(solution)/shard_map/ppermute | solution.py:16
  22.7 33.4 %collective-permute-start.3 = (bf16[128,2048]{0,1:T(8,128)(2,1)S(1)}, bf16[128,2048]{0,1:T(8,128)(2,1)S(1)}, u32[]{:S(2)}, u32[]{:S(2)}) collective-permute-start(bf16[128,2048]{0,1:T(8,128)(2,1)S(1)} %copy.72), channel_id=1, source_target_pairs={{0,1},{1,2},{2,3},{3,4},{4,5},{5,6},{6,7},{7,8},{8,9},{9,10},{10,1... | collective-permute-start | bytes 1572872 | tf_op jit(solution)/shard_map/ppermute | solution.py:16
  25.1 38.7 %copy-start.2 = (pred[128,640]{0,1:T(8,128)(4,1)}, pred[128,640]{0,1:T(8,128)(4,1)S(1)}, u32[]{:S(2)}) copy-start(pred[128,640]{0,1:T(8,128)(4,1)S(1)} %fusion.11) | copy-start | bytes 245764
  56.3 1.5 copy-start.1
  77.2 6.8 %copy-start.3 = (s32[1,2]{1,0:T(1,128)S(1)}, s32[1,2]{1,0:T(1,128)}, u32[]{:S(2)}) copy-start(s32[1,2]{1,0:T(1,128)} %param.8) | copy-start | bytes 28
  77.2 64.1 %all-to-all-start = ((bf16[128,16,512]{0,2,1:T(8,128)(2,1)}), bf16[128,16,512]{0,2,1:T(8,128)(2,1)S(1)}, u32[]{:S(2)}, u32[]{:S(2)}) async-start(bf16[128,16,512]{0,2,1:T(8,128)(2,1)} %bitcast.139), calls=%async_computation | async-start | bytes 4194304 | tf_op jit(solution)/shard_map/all_to_all | solution.py:78
  141.4 1.3 copy-start
  180.6 97.6 %all-to-all-start.1 = ((bf16[16,256,1,512]{3,1,2,0:T(8,128)(2,1)}), bf16[16,256,1,512]{3,1,2,0:T(8,128)(2,1)}, u32[]{:S(2)}, u32[]{:S(2)}) async-start(bf16[16,256,1,512]{3,1,2,0:T(8,128)(2,1)} %fusion.12), calls=%async_computation.1 | async-start | bytes 8388608 | tf_op jit(solution)/shard_map/all_to_all | solution.py:40
